TPU v7x, 512 devices: a whole 4x4x16 slice. The times are simulated.
512 devices in a mesh: head: 16 (over z), ctx: 32 (over x, y, core).
Axes of the slice: x: 4, y: 4, z: 16, core: 2. Of those that a mesh axis runs over, the one named last changes fastest.
Arguments:
- x_mant: bfloat16 [4096, 16384], P('ctx', 'head'), may hold values from -4 to 4
- x_codes: int32 [4096, 512], P('ctx', 'head'), may hold values from -2 to 2
- bc_raw: bfloat16 [4096, 2048], P('ctx'), may hold values from -5 to 5
- gate_z: bfloat16 [4096, 16384], P('ctx', 'head'), may hold values from -5 to 5
- conv_x: float32 [4, 16384], P(None, 'head'), may hold values from -3 to 3
- conv_bc: float32 [4, 2048], replicated, may hold values from -3 to 3
- dt_raw: float32 [4096, 256], P('ctx', 'head'), may hold values from -4 to 4
- a_log: float32 [256], P('head'), as said below
- d_skip: float32 [256], P('head'), may hold values from 0.5 to 1.5
- norm_gain: float32 [16384], P('head'), may hold values from 0.5 to 1.5
- prompt_lengths: int32 [4], replicated, may hold values from 1 to 2112, 4096 in all
- cache_slot: int32 [4], replicated, may hold values from 0 to 63, as said below
- prefix_state: bfloat16 [64, 16384, 128], P('ctx', 'head'), may hold values from -5 to 5
- tail_x: bfloat16 [64, 3, 16384], P('ctx', None, 'head'), may hold values from -5 to 5
- tail_bc: bfloat16 [64, 3, 2048], P('ctx'), may hold values from -5 to 5
Outputs:
- mixed: bfloat16 [4096, 16384], P('ctx', 'head')
Inputs may be any that keep to these rules, and one draw needn't show every extreme that they name: `prompt_lengths`: the lengths sum to 4096, and the longest is exactly 2112. `cache_slot`: slot 63 is read by some prompt and slot 0 by another; prompts may share a slot. `a_log`: log of a positive rate per head.
All inputs are finite; a program needn't handle non-finite values.
Results may differ from a plain program's by a relative error of at most 0.0065.
Values may be sent and summed in bfloat16 or wider, within the bound.
No kernel may reach another device: no remote copies, remote signals or barrier semaphores. Data moves between devices by JAX's collectives and lax.ppermute only.
A program may use at most 64 MiB of HBM per device.

v0:
```python
import jax
import jax.numpy as jnp
from jax import lax
from jax.sharding import PartitionSpec as P

HEADS = 256
GROUPS = 8
eps_norm = 1e-05


def passed_along(array, axis, by):
    devices = lax.axis_size(axis)
    pairs = [(i, i + by) for i in range(devices) if 0 <= i + by < devices]
    return lax.ppermute(array, axis, pairs)


def from_root(value, axis, source):
    kept = jnp.where(lax.axis_index(axis) == source, value, 0).astype(value.dtype)
    return lax.psum(kept, axis)


def entering(array, axis, combine, identity):
    devices, index = (lax.axis_size(axis), lax.axis_index(axis))
    everything = jax.tree.map(lambda part: lax.all_gather(part, axis), array)
    start = jax.tree.map(
        lambda part, zero: jnp.broadcast_to(jnp.asarray(zero, part.dtype), part.shape),
        array,
        identity,
    )

    def hop(k, before):
        reached = k < index
        new = combine(before, jax.tree.map(lambda part: part[k], everything))
        return jax.tree.map(lambda a, b: jnp.where(reached, a, b), new, before)

    return lax.fori_loop(0, devices, hop, start)


def dequant(mantissa, codes):
    row_count, chan_count = mantissa.shape
    block_count = codes.shape[1]
    scaled = mantissa.astype(jnp.float32).reshape(row_count, block_count, chan_count // block_count)
    scaled = scaled * jnp.exp2(codes.astype(jnp.float32))[:, :, None]
    return scaled.reshape(row_count, chan_count)


def prompt_rows(starts, offset, row_count):
    position = jnp.arange(row_count, dtype=jnp.int32) + offset
    inside = (position[:, None] >= starts[None, :]).astype(jnp.int32)
    return jnp.sum(inside, axis=1) - 1


def pick_rows(table, prompt_id):
    hit = prompt_id[:, None] == jnp.arange(table.shape[0], dtype=jnp.int32)[None, :]
    return jnp.sum(jnp.where(hit, table[None, :], 0), axis=1)


def causal_conv(current, previous, tails, weights, prompt_id, start_loc):
    row_count, chan_count = current.shape
    lag_count = previous.shape[0]
    prompt_count = tails.shape[0]
    extended = jnp.concatenate([previous, current], axis=0)
    flat_tails = tails.reshape(prompt_count * lag_count, chan_count)
    row_start = pick_rows(start_loc, prompt_id)
    position = jnp.arange(row_count, dtype=jnp.int32)
    total = jnp.zeros((row_count, chan_count), jnp.float32)
    for shift_by in range(lag_count + 1):
        source = extended[lag_count - shift_by : lag_count - shift_by + row_count]
        earlier = position - shift_by
        index = prompt_id * lag_count + jnp.clip(earlier - row_start + lag_count, 0, lag_count - 1)
        tail_rows = jnp.take(flat_tails, index, axis=0)
        value = jnp.where((earlier < row_start)[:, None], tail_rows, source)
        total = total + weights[lag_count - shift_by][None, :] * value
    return total


def span_local(x_act, b_act, c_act, delta, log_decay, prompt_id, start_loc, prefixes):
    row_count, head_count, width = x_act.shape
    group_count, state = (b_act.shape[1], b_act.shape[2])
    per_group = head_count // group_count
    cumul = jnp.cumsum(log_decay, axis=0)
    before_sum = cumul - log_decay
    position = jnp.arange(row_count, dtype=jnp.int32)
    live = (prompt_id[:, None] == prompt_id[None, :]) & (position[:, None] >= position[None, :])
    scores = jnp.einsum("tgn,sgn->gts", c_act, b_act, preferred_element_type=jnp.float32)

    def one_head(head):
        score = lax.dynamic_index_in_dim(scores, head // per_group, 0, keepdims=False)
        level = lax.dynamic_index_in_dim(cumul, head, 1, keepdims=False)
        stride = lax.dynamic_index_in_dim(delta, head, 1, keepdims=False)
        values = lax.dynamic_index_in_dim(x_act, head, 1, keepdims=False)
        spread = jnp.where(live, level[:, None] - level[None, :], 0.0)
        weights = jnp.where(live, score * jnp.exp(spread) * stride[None, :], 0.0).astype(
            jnp.bfloat16
        )
        return jnp.dot(weights, values, preferred_element_type=jnp.float32)

    intra = lax.map(one_head, jnp.arange(head_count, dtype=jnp.int32))
    intra = jnp.transpose(intra, (1, 0, 2))
    last_prompt = prompt_id[row_count - 1]
    final = cumul[row_count - 1]
    keep = (prompt_id == last_prompt)[:, None]
    fade = jnp.where(keep, jnp.exp(jnp.where(keep, final[None, :] - cumul, 0.0)), 0.0)
    inputs = (x_act.astype(jnp.float32) * (delta * fade)[:, :, None]).astype(jnp.bfloat16)
    grouped = inputs.reshape(row_count, group_count, per_group, width)
    ends = jnp.einsum("sgkp,sgn->gkpn", grouped, b_act, preferred_element_type=jnp.float32)
    ends = ends.reshape(head_count, width, state)
    last_start = lax.dynamic_index_in_dim(start_loc, last_prompt, 0, keepdims=False)
    inside = last_start >= 0
    base = lax.dynamic_index_in_dim(
        before_sum, jnp.clip(last_start, 0, row_count - 1), 0, keepdims=False
    )
    carry_in = jnp.exp(jnp.where(inside, final - base, 0.0))
    prefix_last = lax.dynamic_index_in_dim(prefixes, last_prompt, 0, keepdims=False)
    ends = ends + jnp.where(inside, carry_in[:, None, None] * prefix_last, 0.0)
    opens = jnp.any((start_loc >= 0) & (start_loc < row_count))
    through = jnp.where(opens, 0.0, jnp.exp(final))
    return (intra, ends, through, cumul, before_sum)


def span_init(c_act, incoming, prefixes, prompt_id, start_loc, cumul, before_sum):
    row_count, group_count, state = c_act.shape
    prompt_count, head_count, width = (prefixes.shape[0], prefixes.shape[1], prefixes.shape[2])
    per_group = head_count // group_count
    c_wide = c_act.astype(jnp.float32)
    total = jnp.zeros((row_count, head_count, width), jnp.float32)
    for prompt in range(prompt_count):
        begin = start_loc[prompt]
        start_state = jnp.where(begin >= 0, prefixes[prompt], incoming)
        grouped = start_state.reshape(group_count, per_group, width, state)
        reads = jnp.einsum("tgn,gkpn->tgkp", c_wide, grouped, precision=lax.Precision.HIGHEST)
        reads = reads.reshape(row_count, head_count, width)
        base = lax.dynamic_index_in_dim(
            before_sum, jnp.clip(begin, 0, row_count - 1), 0, keepdims=False
        )
        member = (prompt_id == prompt)[:, None]
        fade = jnp.where(member, jnp.exp(jnp.where(member, cumul - base[None, :], 0.0)), 0.0)
        total = total + fade[:, :, None] * reads
    return total


def combine_states(earlier, later):
    return (earlier[0] * later[0], later[0][:, None, None] * earlier[1] + later[1])


def on_device(
    x_mant,
    x_codes,
    bc_raw,
    gate_z,
    conv_x,
    conv_bc,
    dt_raw,
    a_log,
    d_skip,
    norm_gain,
    prompt_lengths,
    cache_slot,
    prefix_state,
    tail_x,
    tail_bc,
):
    row_count = x_mant.shape[0]
    head_count = a_log.shape[0]
    width = x_mant.shape[1] // head_count
    state = prefix_state.shape[2]
    slot_count = prefix_state.shape[0]
    lag_count = tail_x.shape[1]
    prompt_count = prompt_lengths.shape[0]
    heads_group = HEADS // GROUPS
    group_here = max(1, head_count // heads_group)
    per_group = head_count // group_here
    group_cols = GROUPS * state
    ctx_place = lax.axis_index("ctx")
    head_place = lax.axis_index("head")
    offset = ctx_place * row_count
    first_group = head_place * head_count // heads_group
    starts = jnp.cumsum(prompt_lengths) - prompt_lengths
    start_loc = starts - offset
    prompt_id = prompt_rows(starts, offset, row_count)
    x_wide = dequant(x_mant, x_codes)
    x_exact = x_wide.astype(jnp.bfloat16)
    b_first = first_group * state
    c_first = group_cols + first_group * state
    take_cols = group_here * state
    bc_here = jnp.concatenate(
        [
            lax.dynamic_slice_in_dim(bc_raw, b_first, take_cols, 1),
            lax.dynamic_slice_in_dim(bc_raw, c_first, take_cols, 1),
        ],
        axis=1,
    )
    weight_bc = jnp.concatenate(
        [
            lax.dynamic_slice_in_dim(conv_bc, b_first, take_cols, 1),
            lax.dynamic_slice_in_dim(conv_bc, c_first, take_cols, 1),
        ],
        axis=1,
    )
    tail_here = jnp.concatenate(
        [
            lax.dynamic_slice_in_dim(tail_bc, b_first, take_cols, 2),
            lax.dynamic_slice_in_dim(tail_bc, c_first, take_cols, 2),
        ],
        axis=2,
    )
    previous_x, previous_bc = passed_along(
        (x_exact[row_count - lag_count :], bc_here[row_count - lag_count :]), "ctx", 1
    )

    def fetch_one(prompt, buffer_set):
        slot_here = lax.dynamic_index_in_dim(cache_slot, prompt, 0, keepdims=False)
        owner_rank = slot_here // slot_count
        local_index = slot_here % slot_count
        pieces = (
            lax.dynamic_index_in_dim(prefix_state, local_index, 0, keepdims=False),
            lax.dynamic_index_in_dim(tail_x, local_index, 0, keepdims=False),
            lax.dynamic_index_in_dim(tail_here, local_index, 0, keepdims=False),
        )
        arrived = (
            from_root(pieces[0], "ctx", owner_rank),
            from_root(pieces[1], "ctx", owner_rank),
            from_root(pieces[2], "ctx", owner_rank),
        )
        return tuple(
            (
                lax.dynamic_update_index_in_dim(holder, piece, prompt, 0)
                for holder, piece in zip(buffer_set, arrived)
            )
        )

    empty_set = (
        jnp.zeros((prompt_count,) + prefix_state.shape[1:], jnp.bfloat16),
        jnp.zeros((prompt_count,) + tail_x.shape[1:], jnp.bfloat16),
        jnp.zeros((prompt_count,) + tail_here.shape[1:], jnp.bfloat16),
    )
    fetched_state, fetched_x, fetched_bc = lax.fori_loop(0, prompt_count, fetch_one, empty_set)
    prefixes = fetched_state.astype(jnp.float32).reshape(prompt_count, head_count, width, state)
    tails_x = fetched_x.astype(jnp.float32)
    tails_bc = fetched_bc.astype(jnp.float32)
    conv_out = causal_conv(
        x_wide, previous_x.astype(jnp.float32), tails_x, conv_x, prompt_id, start_loc
    )
    x_act = jax.nn.silu(conv_out).astype(jnp.bfloat16).reshape(row_count, head_count, width)
    bc_out = causal_conv(
        bc_here.astype(jnp.float32),
        previous_bc.astype(jnp.float32),
        tails_bc,
        weight_bc,
        prompt_id,
        start_loc,
    )
    bc_act = jax.nn.silu(bc_out).astype(jnp.bfloat16)
    b_act = bc_act[:, :take_cols].reshape(row_count, group_here, state)
    c_act = bc_act[:, take_cols:].reshape(row_count, group_here, state)
    delta = jax.nn.softplus(dt_raw)
    log_decay = -jnp.exp(a_log)[None, :] * delta
    intra, ends, through, cumul, before_sum = span_local(
        x_act, b_act, c_act, delta, log_decay, prompt_id, start_loc, prefixes
    )
    identity = (jnp.ones_like(through), jnp.zeros_like(ends))
    _, incoming = entering((through, ends), "ctx", combine_states, identity)
    init = span_init(c_act, incoming, prefixes, prompt_id, start_loc, cumul, before_sum)
    y_full = intra + init + d_skip[None, :, None] * x_act.astype(jnp.float32)
    gated = y_full * jax.nn.silu(gate_z.astype(jnp.float32).reshape(row_count, head_count, width))
    head_squares = jnp.sum(gated * gated, axis=2)
    local_squares = jnp.sum(head_squares.reshape(row_count, group_here, per_group), axis=2)
    all_groups = lax.dynamic_update_slice_in_dim(
        jnp.zeros((row_count, GROUPS), jnp.float32), local_squares, first_group, 1
    )
    summed = lax.psum(all_groups, "head")
    group_totals = lax.dynamic_slice_in_dim(summed, first_group, group_here, 1)
    inverse = lax.rsqrt(group_totals / (heads_group * width) + eps_norm)
    inverse = jnp.repeat(inverse, per_group, axis=1)
    mixed = gated * inverse[:, :, None] * norm_gain.reshape(head_count, width)[None, :, :]
    return mixed.reshape(row_count, head_count * width).astype(jnp.bfloat16)


def solution(mesh):
    in_specs = (
        P("ctx", "head"),
        P("ctx", "head"),
        P("ctx", None),
        P("ctx", "head"),
        P(None, "head"),
        P(),
        P("ctx", "head"),
        P("head"),
        P("head"),
        P("head"),
        P(),
        P(),
        P("ctx", "head", None),
        P("ctx", None, "head"),
        P("ctx", None, None),
    )
    out_specs = P("ctx", "head")
    return jax.shard_map(
        on_device, mesh=mesh, in_specs=in_specs, out_specs=out_specs, check_vma=False
    )
```

profile of v0, /device:TPU:16, one launch (start us, length us, event | category | flops | bytes accessed | tf_op | source)
XLA Modules:
  0.0 829.4 jit_solution(14115373180927704455)
XLA Ops:
  8.2 1.9 collective-permute-start
  12.9 3.3 collective-permute-start.1
  35.3 558.4 %while.44 = (s32[]{:T(128)}, bf16[4,1024,128]{2,1,0:T(8,128)(2,1)S(1)}, bf16[4,3,1024]{2,1,0:T(4,128)(2,1)S(1)}, bf16[4,3,256]{2,1,0:T(4,128)(2,1)S(1)}, s32[4]{...) while((s32[]{:T(128)}, ...), condition=%wide.region_7.8_spmd, body=%wide.region_3.7_spmd.sunk | while | flops 269851 | bytes 2673102 | solution.py:237
  39.2 1.7 dynamic-slice_select_fusion.6
  40.9 116.9 %all-reduce.2 = (bf16[1,3,1024]{2,1,0:T(4,128)(2,1)S(1)}, bf16[1,3,256]{2,1,0:T(4,128)(2,1)S(1)}) all-reduce(bf16[1,3,1024]{2,1,0:T(4,128)(2,1)S(1)} %dynamic-slice_select_fusion.7, bf16[1,3,256]{2,1,0:T(4,128)(2,1)S(1)} %dynamic-slice_select_fusion.8), channel_id=1, replica_groups=mesh['head'=16,'ctx'=32] {'ctx'}, use_global_device_ids=true, to_apply=%region_5.5 | all-reduce | flops 3840 | bytes 15360 | tf_op jit(solution)/shard_map/while/body/eval_jaxpr/psum | solution.py:19
  157.9 19.0 %all-reduce.5.cloned.1.call-done = bf16[1,1024,128]{2,1,0:T(8,128)(2,1)} async-done(((bf16[1,1024,128]{2,1,0:T(8,128)(2,1)}), bf16[1,1024,128]{2,1,0:T(8,128)(2,1)}) %all-reduce.5.cloned.1.call-update) | async-done | bytes 262160 | tf_op jit(solution)/shard_map/while/body/eval_jaxpr/psum | solution.py:19
  181.7 1.7 dynamic-slice_select_fusion.6
  183.5 117.7 %all-reduce.2 = (bf16[1,3,1024]{2,1,0:T(4,128)(2,1)S(1)}, bf16[1,3,256]{2,1,0:T(4,128)(2,1)S(1)}) all-reduce(bf16[1,3,1024]{2,1,0:T(4,128)(2,1)S(1)} %dynamic-slice_select_fusion.7, bf16[1,3,256]{2,1,0:T(4,128)(2,1)S(1)} %dynamic-slice_select_fusion.8), channel_id=1, replica_groups=mesh['head'=16,'ctx'=32] {'ctx'}, use_global_device_ids=true, to_apply=%region_5.5 | all-reduce | flops 3840 | bytes 15360 | tf_op jit(solution)/shard_map/while/body/eval_jaxpr/psum | solution.py:19
  301.2 14.3 %all-reduce.5.cloned.1.call-done = bf16[1,1024,128]{2,1,0:T(8,128)(2,1)} async-done(((bf16[1,1024,128]{2,1,0:T(8,128)(2,1)}), bf16[1,1024,128]{2,1,0:T(8,128)(2,1)}) %all-reduce.5.cloned.1.call-update) | async-done | bytes 262160 | tf_op jit(solution)/shard_map/while/body/eval_jaxpr/psum | solution.py:19
  320.4 1.7 dynamic-slice_select_fusion.6
  322.1 117.7 %all-reduce.2 = (bf16[1,3,1024]{2,1,0:T(4,128)(2,1)S(1)}, bf16[1,3,256]{2,1,0:T(4,128)(2,1)S(1)}) all-reduce(bf16[1,3,1024]{2,1,0:T(4,128)(2,1)S(1)} %dynamic-slice_select_fusion.7, bf16[1,3,256]{2,1,0:T(4,128)(2,1)S(1)} %dynamic-slice_select_fusion.8), channel_id=1, replica_groups=mesh['head'=16,'ctx'=32] {'ctx'}, use_global_device_ids=true, to_apply=%region_5.5 | all-reduce | flops 3840 | bytes 15360 | tf_op jit(solution)/shard_map/while/body/eval_jaxpr/psum | solution.py:19
  439.8 14.3 %all-reduce.5.cloned.1.call-done = bf16[1,1024,128]{2,1,0:T(8,128)(2,1)} async-done(((bf16[1,1024,128]{2,1,0:T(8,128)(2,1)}), bf16[1,1024,128]{2,1,0:T(8,128)(2,1)}) %all-reduce.5.cloned.1.call-update) | async-done | bytes 262160 | tf_op jit(solution)/shard_map/while/body/eval_jaxpr/psum | solution.py:19
  459.0 1.7 dynamic-slice_select_fusion.6
  460.7 117.7 %all-reduce.2 = (bf16[1,3,1024]{2,1,0:T(4,128)(2,1)S(1)}, bf16[1,3,256]{2,1,0:T(4,128)(2,1)S(1)}) all-reduce(bf16[1,3,1024]{2,1,0:T(4,128)(2,1)S(1)} %dynamic-slice_select_fusion.7, bf16[1,3,256]{2,1,0:T(4,128)(2,1)S(1)} %dynamic-slice_select_fusion.8), channel_id=1, replica_groups=mesh['head'=16,'ctx'=32] {'ctx'}, use_global_device_ids=true, to_apply=%region_5.5 | all-reduce | flops 3840 | bytes 15360 | tf_op jit(solution)/shard_map/while/body/eval_jaxpr/psum | solution.py:19
  578.5 14.3 %all-reduce.5.cloned.1.call-done = bf16[1,1024,128]{2,1,0:T(8,128)(2,1)} async-done(((bf16[1,1024,128]{2,1,0:T(8,128)(2,1)}), bf16[1,1024,128]{2,1,0:T(8,128)(2,1)}) %all-reduce.5.cloned.1.call-update) | async-done | bytes 262160 | tf_op jit(solution)/shard_map/while/body/eval_jaxpr/psum | solution.py:19
  595.3 1.6 gather_fusion.4
  596.9 1.6 gather_fusion.5
  599.9 1.6 gather_fusion.6
  602.9 1.6 gather_fusion.7
  608.0 3.8 multiply_convert_fusion.1
  611.7 1.8 copy.93
  613.5 2.0 fusion.31
  627.5 23.4 %all-gather = f32[32,1,16]{2,1,0:T(1,128)} all-gather(f32[1,1,16]{2,1,0:T(1,128)} %get-tuple-element.529), channel_id=1, replica_groups=mesh['head'=16,'ctx'=32] {'ctx'}, dimensions={0}, use_global_device_ids=true | all-gather | bytes 2112 | tf_op jit(solution)/shard_map/all_gather | solution.py:24
  652.3 73.1 %while.45 = (s32[]{:T(128)}, f32[16,128,64]{1,2,0:T(8,128)}, f32[1,128,128]{2,1,0:T(8,128)S(1)}, s32[16]{0:T(128)S(1)}, f32[128,16]{0,1:T(8,128)}, /*index=5*/f3...) while((s32[]{:T(128)}, f32[16,128,64]{1,2,0:T(8,128)}, ...), condition=%wide.region_10.13_spmd.clone, body=%wide.region_9.12_spmd.clone.sunk | while | flops 2244613 | bytes 119971 | solution.py:98
  655.3 1.6 fusion.107
  673.6 1.6 fusion.107
  687.3 1.6 fusion.107
  691.9 1.6 fusion.107
  705.6 1.6 fusion.107
  725.5 59.8 %while.46 = (s32[]{:T(128)}, f32[16,64,128]{2,1,0:T(8,128)S(1)}, s32[]{:T(128)}, f32[32,16]{1,0:T(8,128)}, f32[32,16,64,128]{3,2,1,0:T(8,128)}, /*index=5*/s32[]{:T(128)}, s32[]{:T(128)}) while((s32[]{:T(128)}, f32[16,64,128]{2,1,0:T(8,128)S(1)}, s32[]{:T(128)}, f32[32,16]{1,0:T(8,128)}, f32[32,16,64,128]{3,2,1,0:T(8,128)}, ...), condition=%wide.region_13.16_spmd.clone, body=%wide.region_12.15_spmd.clone.sunk | while | flops 524292 | bytes 1573161 | solution.py:36
  788.2 1.7 multiply_reduce_fusion
  789.9 31.3 %psum.49 = f32[128,8]{0,1:T(8,128)S(1)} all-reduce(f32[128,8]{0,1:T(8,128)S(1)} %dynamic_update_slice.40), channel_id=1, replica_groups=mesh['head'=16,'ctx'=32] {'head'}, use_global_device_ids=true, to_apply=%region_15.18 | all-reduce | flops 1024 | bytes 8192 | tf_op jit(solution)/shard_map/psum | solution.py:271
  (226 shorter events, 146.1 us)
Async XLA Ops:
  8.2 597.6 %collective-permute-start = (bf16[3,256]{1,0:T(4,128)(2,1)S(1)}, bf16[3,256]{1,0:T(4,128)(2,1)S(1)}, u32[]{:S(2)}, u32[]{:S(2)}) collective-permute-start(bf16[3,256]{1,0:T(4,128)(2,1)S(1)} %fusion.77), channel_id=1, source_target_pairs={{0,1},{1,2},{2,3},{3,4},{4,5},{5,6},{6,7},{7,8},{8,9},{9,10},{10,1... | collective-permute-start | bytes 4616 | tf_op jit(solution)/shard_map/ppermute | solution.py:14
  12.1 0.8 copy-start
  12.9 594.4 %collective-permute-start.1 = (bf16[3,1024]{1,0:T(4,128)(2,1)}, bf16[3,1024]{1,0:T(4,128)(2,1)}, u32[]{:S(2)}, u32[]{:S(2)}) collective-permute-start(bf16[3,1024]{1,0:T(4,128)(2,1)} %slice.281), channel_id=1, source_target_pairs={{0,1},{1,2},{2,3},{3,4},{4,5},{5,6},{6,7},{7,8},{8,9},{9,10},{10,1... | collective-permute-start | bytes 18440 | tf_op jit(solution)/shard_map/ppermute | solution.py:14
  19.1 5.1 copy-start.3
  35.3 141.5 %all-reduce.5.cloned.1.call-start = ((), (), s32[]{:S(2)}) async-start(), calls=%async_computation.1 | async-start | bytes 524288 | tf_op jit(solution)/shard_map/while/body/eval_jaxpr/psum | solution.py:19
  177.8 137.6 %all-reduce.5.cloned.1.call-start = ((), (), s32[]{:S(2)}) async-start(), calls=%async_computation.1 | async-start | bytes 524288 | tf_op jit(solution)/shard_map/while/body/eval_jaxpr/psum | solution.py:19
  316.5 137.6 %all-reduce.5.cloned.1.call-start = ((), (), s32[]{:S(2)}) async-start(), calls=%async_computation.1 | async-start | bytes 524288 | tf_op jit(solution)/shard_map/while/body/eval_jaxpr/psum | solution.py:19
  455.1 137.6 %all-reduce.5.cloned.1.call-start = ((), (), s32[]{:S(2)}) async-start(), calls=%async_computation.1 | async-start | bytes 524288 | tf_op jit(solution)/shard_map/while/body/eval_jaxpr/psum | solution.py:19
  593.7 131.7 %all-gather.3.cloned.1.call-start = ((), (), s32[]{:S(2)}) async-start(), calls=%async_computation | async-start | bytes 17301504 | tf_op jit(solution)/shard_map/all_gather | solution.py:24
  652.3 168.9 %copy-start.2 = (f32[16,64]{1,0:T(8,128)S(1)}, f32[16,64]{1,0:T(8,128)}, u32[]{:S(2)}) copy-start(f32[16,64]{1,0:T(8,128)} %mul.333) | copy-start | bytes 12292
  725.4 62.7 %copy-start.1 = (bf16[128,16,64]{0,2,1:T(8,128)(2,1)}, bf16[128,16,64]{0,2,1:T(8,128)(2,1)S(1)}, u32[]{:S(2)}) copy-start(bf16[128,16,64]{0,2,1:T(8,128)(2,1)S(1)} %get-tuple-element.805) | copy-start | bytes 786436
Sparse Core Ops, SparseCore 0:
  41.0 135.7 all-reduce.4
  183.6 131.8 all-reduce.4
  322.2 131.8 all-reduce.4
  460.8 131.8 all-reduce.4
Sparse Core Ops, SparseCore 1:
  615.6 87.8 all-gather.2
where the time goes:
time: 835 us; the launch traced here: 829 us
  blocking collectives  525 us (63%)
  local copies, waits for them, and re-layouts  83.4 us (10%)
  waiting for transfers between devices  61.8 us (7%)
  other arithmetic  60.6 us (7%)
  loops' own time  38.6 us (5%)
  matrix products  32 us (4%)
  between operations  23 us (3%)
    psum x4, blocking collectives, from_root(): return lax.psum(kept, axis)  470 us
    psum x4, waiting for transfers between devices, from_root(): return lax.psum(kept, axis)  61.7 us
    select_n x32, other arithmetic, hop(): return jax.tree.map(lambda a, b: jnp.where(reached, a, b), new, before)  37.4 us
    psum x1, blocking collectives, on_device(): summed = lax.psum(all_groups, 'head')  31.3 us
    another operation x1, loops' own time, span_local(): intra = lax.map(one_head, jnp.arange(head_count, dtype=jnp.int32))  27.3 us
    dot_general x16, matrix products, one_head(): return jnp.dot(weights, values, preferred_element_type=jnp.float32)  25.3 us
    all_gather x1, blocking collectives, entering(): everything = jax.tree.map(lambda part: lax.all_gather(part, axis), array)  23.4 us
    mul x32, local copies, waits for them, and re-layouts, combine_states(): later[0][:, None, None] * earlier[1] + later[1]  21.8 us
  transfers between devices with their start and end apart: 7, of which 4 were waited for; matrix products, arithmetic and copies ran while one was open for 12% of the time, Pallas kernels for 0%

commit v1 on v0

--- a/solution.py
+++ b/solution.py
@@ -16,7 +16,7 @@
 
 def from_root(value, axis, source):
     kept = jnp.where(lax.axis_index(axis) == source, value, 0).astype(value.dtype)
-    return lax.psum(kept, axis)
+    return jnp.sum(lax.all_gather(kept, axis), axis=0)
 
 
 def entering(array, axis, combine, identity):

time: 835 us -> 593 us (0.71)
  the two profiles are of different devices: /device:TPU:16 before, /device:TPU:2 now
where the time goes in v1:
time: 593 us; the launch traced here: 588 us
  blocking collectives  239 us (40%)
  waiting for transfers between devices  91.5 us (15%)
  other arithmetic  80.6 us (14%)
  local copies, waits for them, and re-layouts  79.9 us (13%)
  loops' own time  38.2 us (6%)
  matrix products  30.5 us (5%)
  between operations  23.2 us (4%)
    all_gather x8, blocking collectives, from_root(): return jnp.sum(lax.all_gather(kept, axis), axis=0)  185 us
    all_gather x4, waiting for transfers between devices, from_root(): return jnp.sum(lax.all_gather(kept, axis), axis=0)  91.4 us
    select_n x32, other arithmetic, hop(): return jax.tree.map(lambda a, b: jnp.where(reached, a, b), new, before)  37.4 us
    psum x1, blocking collectives, on_device(): summed = lax.psum(all_groups, 'head')  31.3 us
    another operation x1, loops' own time, span_local(): intra = lax.map(one_head, jnp.arange(head_count, dtype=jnp.int32))  26.9 us
    dot_general x16, matrix products, one_head(): return jnp.dot(weights, values, preferred_element_type=jnp.float32)  24.9 us
    all_gather x1, blocking collectives, entering(): everything = jax.tree.map(lambda part: lax.all_gather(part, axis), array)  22.3 us
    mul x32, local copies, waits for them, and re-layouts, combine_states(): later[0][:, None, None] * earlier[1] + later[1]  22 us
  transfers between devices with their start and end apart: 7, of which 4 were waited for; matrix products, arithmetic and copies ran while one was open for 20% of the time, Pallas kernels for 0%

profile of v1, /device:TPU:2, one launch (start us, length us, event | category | flops | bytes accessed | tf_op | source)
XLA Modules:
  0.0 588.1 jit_solution(11985059383814895099)
XLA Ops:
  8.2 1.9 collective-permute-start
  12.9 3.6 collective-permute-start.1
  36.0 319.0 %while.45 = (s32[]{:T(128)}, bf16[4,1024,128]{2,1,0:T(8,128)(2,1)S(1)}, bf16[4,3,1024]{2,1,0:T(4,128)(2,1)S(1)}, bf16[4,3,256]{2,1,0:T(4,128)(2,1)S(1)}, s32[4]{...) while((s32[]{:T(128)}, ...), condition=%wide.region_7.8_spmd, body=%wide.region_3.7_spmd.sunk | while | flops 4317211 | bytes 36194772 | solution.py:237
  39.9 1.7 dynamic-slice_select_fusion.6
  41.6 25.3 %all_gather.56 = bf16[32,3,1024]{2,1,0:T(4,128)(2,1)S(1)} all-gather(bf16[1,3,1024]{2,1,0:T(4,128)(2,1)S(1)} %dynamic-slice_select_fusion.7), channel_id=1, replica_groups=mesh['head'=16,'ctx'=32] {'ctx'}, dimensions={0}, use_global_device_ids=true | all-gather | bytes 202752 | tf_op jit(solution)/shard_map/while/body/eval_jaxpr/all_gather | solution.py:19
  67.0 21.5 %all_gather.57 = bf16[32,3,256]{2,1,0:T(4,128)(2,1)S(1)} all-gather(bf16[1,3,256]{2,1,0:T(4,128)(2,1)S(1)} %dynamic-slice_select_fusion.8), channel_id=1, replica_groups=mesh['head'=16,'ctx'=32] {'ctx'}, dimensions={0}, use_global_device_ids=true | all-gather | bytes 50688 | tf_op jit(solution)/shard_map/while/body/eval_jaxpr/all_gather | solution.py:19
  88.6 25.7 %all-gather.6.cloned.1.call-done = bf16[32,1024,128]{2,1,0:T(8,128)(2,1)} async-done(((bf16[1,1024,128]{2,1,0:T(8,128)(2,1)}), bf16[32,1024,128]{2,1,0:T(8,128)(2,1)}) %all-gather.6.cloned.1.call-update) | async-done | bytes 8388624 | tf_op jit(solution)/shard_map/while/body/eval_jaxpr/all_gather | solution.py:19
  114.3 4.7 reduce_sum.89
  123.0 1.7 dynamic-slice_select_fusion.6
  124.7 23.2 %all_gather.56 = bf16[32,3,1024]{2,1,0:T(4,128)(2,1)S(1)} all-gather(bf16[1,3,1024]{2,1,0:T(4,128)(2,1)S(1)} %dynamic-slice_select_fusion.7), channel_id=1, replica_groups=mesh['head'=16,'ctx'=32] {'ctx'}, dimensions={0}, use_global_device_ids=true | all-gather | bytes 202752 | tf_op jit(solution)/shard_map/while/body/eval_jaxpr/all_gather | solution.py:19
  148.0 22.9 %all_gather.57 = bf16[32,3,256]{2,1,0:T(4,128)(2,1)S(1)} all-gather(bf16[1,3,256]{2,1,0:T(4,128)(2,1)S(1)} %dynamic-slice_select_fusion.8), channel_id=1, replica_groups=mesh['head'=16,'ctx'=32] {'ctx'}, dimensions={0}, use_global_device_ids=true | all-gather | bytes 50688 | tf_op jit(solution)/shard_map/while/body/eval_jaxpr/all_gather | solution.py:19
  171.0 21.9 %all-gather.6.cloned.1.call-done = bf16[32,1024,128]{2,1,0:T(8,128)(2,1)} async-done(((bf16[1,1024,128]{2,1,0:T(8,128)(2,1)}), bf16[32,1024,128]{2,1,0:T(8,128)(2,1)}) %all-gather.6.cloned.1.call-update) | async-done | bytes 8388624 | tf_op jit(solution)/shard_map/while/body/eval_jaxpr/all_gather | solution.py:19
  192.9 4.7 reduce_sum.89
  201.7 1.7 dynamic-slice_select_fusion.6
  203.4 23.2 %all_gather.56 = bf16[32,3,1024]{2,1,0:T(4,128)(2,1)S(1)} all-gather(bf16[1,3,1024]{2,1,0:T(4,128)(2,1)S(1)} %dynamic-slice_select_fusion.7), channel_id=1, replica_groups=mesh['head'=16,'ctx'=32] {'ctx'}, dimensions={0}, use_global_device_ids=true | all-gather | bytes 202752 | tf_op jit(solution)/shard_map/while/body/eval_jaxpr/all_gather | solution.py:19
  226.7 22.9 %all_gather.57 = bf16[32,3,256]{2,1,0:T(4,128)(2,1)S(1)} all-gather(bf16[1,3,256]{2,1,0:T(4,128)(2,1)S(1)} %dynamic-slice_select_fusion.8), channel_id=1, replica_groups=mesh['head'=16,'ctx'=32] {'ctx'}, dimensions={0}, use_global_device_ids=true | all-gather | bytes 50688 | tf_op jit(solution)/shard_map/while/body/eval_jaxpr/all_gather | solution.py:19
  249.7 21.9 %all-gather.6.cloned.1.call-done = bf16[32,1024,128]{2,1,0:T(8,128)(2,1)} async-done(((bf16[1,1024,128]{2,1,0:T(8,128)(2,1)}), bf16[32,1024,128]{2,1,0:T(8,128)(2,1)}) %all-gather.6.cloned.1.call-update) | async-done | bytes 8388624 | tf_op jit(solution)/shard_map/while/body/eval_jaxpr/all_gather | solution.py:19
  271.6 4.7 reduce_sum.89
  280.3 1.7 dynamic-slice_select_fusion.6
  282.0 23.2 %all_gather.56 = bf16[32,3,1024]{2,1,0:T(4,128)(2,1)S(1)} all-gather(bf16[1,3,1024]{2,1,0:T(4,128)(2,1)S(1)} %dynamic-slice_select_fusion.7), channel_id=1, replica_groups=mesh['head'=16,'ctx'=32] {'ctx'}, dimensions={0}, use_global_device_ids=true | all-gather | bytes 202752 | tf_op jit(solution)/shard_map/while/body/eval_jaxpr/all_gather | solution.py:19
  305.4 22.9 %all_gather.57 = bf16[32,3,256]{2,1,0:T(4,128)(2,1)S(1)} all-gather(bf16[1,3,256]{2,1,0:T(4,128)(2,1)S(1)} %dynamic-slice_select_fusion.8), channel_id=1, replica_groups=mesh['head'=16,'ctx'=32] {'ctx'}, dimensions={0}, use_global_device_ids=true | all-gather | bytes 50688 | tf_op jit(solution)/shard_map/while/body/eval_jaxpr/all_gather | solution.py:19
  328.3 21.9 %all-gather.6.cloned.1.call-done = bf16[32,1024,128]{2,1,0:T(8,128)(2,1)} async-done(((bf16[1,1024,128]{2,1,0:T(8,128)(2,1)}), bf16[32,1024,128]{2,1,0:T(8,128)(2,1)}) %all-gather.6.cloned.1.call-update) | async-done | bytes 8388624 | tf_op jit(solution)/shard_map/while/body/eval_jaxpr/all_gather | solution.py:19
  350.2 4.7 reduce_sum.89
  356.7 1.6 gather_fusion.4
  369.3 4.0 multiply_convert_fusion.1
  373.2 1.8 copy.91
  375.0 2.0 fusion.31
  389.0 22.3 %all-gather = f32[32,1,16]{2,1,0:T(1,128)} all-gather(f32[1,1,16]{2,1,0:T(1,128)} %get-tuple-element.543), channel_id=1, replica_groups=mesh['head'=16,'ctx'=32] {'ctx'}, dimensions={0}, use_global_device_ids=true | all-gather | bytes 2112 | tf_op jit(solution)/shard_map/all_gather | solution.py:24
  412.7 72.3 %while.46 = (s32[]{:T(128)}, f32[16,128,64]{1,2,0:T(8,128)}, f32[1,128,128]{2,1,0:T(8,128)S(1)}, s32[16]{0:T(128)S(1)}, f32[128,16]{0,1:T(8,128)}, /*index=5*/f3...) while((s32[]{:T(128)}, f32[16,128,64]{1,2,0:T(8,128)}, ...), condition=%wide.region_10.13_spmd.clone, body=%wide.region_9.12_spmd.clone.sunk | while | flops 2244613 | bytes 119971 | solution.py:98
  485.0 60.0 %while.47 = (s32[]{:T(128)}, f32[16,64,128]{2,1,0:T(8,128)S(1)}, s32[]{:T(128)}, f32[32,16]{1,0:T(8,128)}, f32[32,16,64,128]{3,2,1,0:T(8,128)}, /*index=5*/s32[]{:T(128)}, s32[]{:T(128)}) while((s32[]{:T(128)}, f32[16,64,128]{2,1,0:T(8,128)S(1)}, s32[]{:T(128)}, f32[32,16]{1,0:T(8,128)}, f32[32,16,64,128]{3,2,1,0:T(8,128)}, ...), condition=%wide.region_13.16_spmd.clone, body=%wide.region_12.15_spmd.clone.sunk | while | flops 524292 | bytes 1573161 | solution.py:36
  546.9 1.7 multiply_reduce_fusion
  548.6 31.3 %psum.7 = f32[128,8]{0,1:T(8,128)S(1)} all-reduce(f32[128,8]{0,1:T(8,128)S(1)} %dynamic_update_slice.43), channel_id=1, replica_groups=mesh['head'=16,'ctx'=32] {'head'}, use_global_device_ids=true, to_apply=%region_15.18 | all-reduce | flops 1024 | bytes 8192 | tf_op jit(solution)/shard_map/psum | solution.py:271
  (246 shorter events, 154.6 us)
Async XLA Ops:
  8.2 358.9 %collective-permute-start = (bf16[3,256]{1,0:T(4,128)(2,1)S(1)}, bf16[3,256]{1,0:T(4,128)(2,1)S(1)}, u32[]{:S(2)}, u32[]{:S(2)}) collective-permute-start(bf16[3,256]{1,0:T(4,128)(2,1)S(1)} %fusion.77), channel_id=1, source_target_pairs={{0,1},{1,2},{2,3},{3,4},{4,5},{5,6},{6,7},{7,8},{8,9},{9,10},{10,1... | collective-permute-start | bytes 4616 | tf_op jit(solution)/shard_map/ppermute | solution.py:14
  12.1 0.8 copy-start
  12.9 355.6 %collective-permute-start.1 = (bf16[3,1024]{1,0:T(4,128)(2,1)}, bf16[3,1024]{1,0:T(4,128)(2,1)}, u32[]{:S(2)}, u32[]{:S(2)}) collective-permute-start(bf16[3,1024]{1,0:T(4,128)(2,1)} %slice.281), channel_id=1, source_target_pairs={{0,1},{1,2},{2,3},{3,4},{4,5},{5,6},{6,7},{7,8},{8,9},{9,10},{10,1... | collective-permute-start | bytes 18440 | tf_op jit(solution)/shard_map/ppermute | solution.py:14
  19.4 5.4 copy-start.5
  36.0 78.2 %all-gather.6.cloned.1.call-start = ((), (), s32[]{:S(2)}) async-start(), calls=%async_computation.1 | async-start | bytes 8650752 | tf_op jit(solution)/shard_map/while/body/eval_jaxpr/all_gather | solution.py:19
  119.1 73.8 %all-gather.6.cloned.1.call-start = ((), (), s32[]{:S(2)}) async-start(), calls=%async_computation.1 | async-start | bytes 8650752 | tf_op jit(solution)/shard_map/while/body/eval_jaxpr/all_gather | solution.py:19
  197.7 73.8 %all-gather.6.cloned.1.call-start = ((), (), s32[]{:S(2)}) async-start(), calls=%async_computation.1 | async-start | bytes 8650752 | tf_op jit(solution)/shard_map/while/body/eval_jaxpr/all_gather | solution.py:19
  276.4 73.8 %all-gather.6.cloned.1.call-start = ((), (), s32[]{:S(2)}) async-start(), calls=%async_computation.1 | async-start | bytes 8650752 | tf_op jit(solution)/shard_map/while/body/eval_jaxpr/all_gather | solution.py:19
  355.1 129.9 %all-gather.4.cloned.1.call-start = ((), (), s32[]{:S(2)}) async-start(), calls=%async_computation | async-start | bytes 17301504 | tf_op jit(solution)/shard_map/all_gather | solution.py:24
  412.3 132.6 %copy-start.1 = (f32[1,1024,128]{2,1,0:T(8,128)S(1)}, f32[1,1024,128]{2,1,0:T(8,128)}, u32[]{:S(2)}) copy-start(f32[1,1024,128]{2,1,0:T(8,128)} %get-tuple-element.527) | copy-start | bytes 1572868
  412.7 132.3 %copy-start.3 = (f32[128,16]{0,1:T(8,128)S(1)}, f32[128,16]{0,1:T(8,128)}, u32[]{:S(2)}) copy-start(f32[128,16]{0,1:T(8,128)} %copy.92) | copy-start | bytes 24580
  485.0 60.0 %copy-start.2 = (bf16[128,16,64]{0,2,1:T(8,128)(2,1)}, bf16[128,16,64]{0,2,1:T(8,128)(2,1)S(1)}, u32[]{:S(2)}) copy-start(bf16[128,16,64]{0,2,1:T(8,128)(2,1)S(1)} %get-tuple-element.818) | copy-start | bytes 786436
  485.0 95.0 %copy-start.4 = (f32[16,64]{1,0:T(8,128)S(1)}, f32[16,64]{1,0:T(8,128)}, u32[]{:S(2)}) copy-start(f32[16,64]{1,0:T(8,128)} %mul.333) | copy-start | bytes 12292
Sparse Core Ops, SparseCore 0:
  41.7 72.5 all-gather.5
  124.8 68.0 all-gather.5
  203.5 68.0 all-gather.5
  282.1 68.0 all-gather.5
Sparse Core Ops, SparseCore 1:
  377.1 87.5 all-gather.3
